TPU v7x, 512 devices: a whole 4x8x8 slice. The times are simulated.
512 devices in a mesh: rows: 8 (over z_lo, core), vec: 64 (over x, y, z_hi).
Axes of the slice: x: 4, y: 8, z: 8 (z_hi: 2, z_lo: 4; z = z_hi * 4 + z_lo), core: 2. Of those that a mesh axis runs over, the one named last changes fastest.
Arguments:
- vectors: float32 [512, 32768], P('vec', 'rows'), may hold values from -6 to 6
- tile_table: float32 [16, 128, 128], replicated, may hold values from -0.3125 to 0.3125
- offsets: int32 [256, 3], P('rows'), may hold values from -2 to 2, as said below
- tile_ids: int32 [256, 3], P('rows'), may hold values from 0 to 15
- bounds: float32 [3], replicated, may hold values from -1.9 to 2.3, as said below
Outputs:
- filtered: float32 [512, 32768], P('vec', 'rows')
- gram_matrix: float32 [512, 512], P(('rows', 'vec'))
Inputs may be any that keep to these rules, and one draw needn't show every extreme that they name: offsets[j, 0] is 0 for every row block j; wherever offsets[j, s] = o is not 0 and j + o lies in 0..255, row block j + o has a slot with offset -o and the same tile number, so the Hamiltonian is symmetric. bounds[0] < bounds[1] < bounds[2]; bounds[1] - bounds[0] lies between 0.1 and 0.3, bounds[2] - bounds[1] between 3.0 and 3.6, and bounds[1] + bounds[2] between 0.4 and 1.0.
All inputs are finite; a program needn't handle non-finite values.
Results may differ from a plain program's by a relative error of at most 0.00013.
Values sent between devices are 32-bit elements; how exact they have to be, the bound alone decides.
No kernel may reach another device: no remote copies, remote signals or barrier semaphores. Data moves between devices by JAX's collectives and lax.ppermute only.
A program may use at most 64 MiB of HBM per device.

v0:
```python
import jax
import jax.numpy as jnp
from jax import lax
from jax.sharding import PartitionSpec as P

BLOCK = 128
R = 2
STEPS = 4


def extended_2(array, sides, width):
    for axis, dim in sides:
        size, length = (lax.axis_size(axis), array.shape[dim])
        up = [(i, (i + 1) % size) for i in range(size - 1)]
        down = [(j, i) for i, j in up]
        last = lax.slice_in_dim(array, length - width, length, axis=dim)
        first = lax.slice_in_dim(array, 0, width, axis=dim)
        before = lax.ppermute(last, axis, up)
        after = lax.ppermute(first, axis, down)
        array = jnp.concatenate([before, array, after], axis=dim)
    return array


def band_product(extended, variant_table, metadata, first_block, out_blocks):
    ext_width = extended.shape[0]
    distinct = variant_table.shape[0] // 3
    slot_count = metadata.shape[1] // 2
    block_shift = metadata[first_block : first_block + out_blocks, :slot_count]
    tile_choice = metadata[first_block : first_block + out_blocks, slot_count:]
    tile_kind = jnp.where(block_shift > 0, 0, jnp.where(block_shift < 0, 1, 2)).astype(jnp.int32)
    table_index = tile_choice + distinct * tile_kind
    positions = first_block + jnp.arange(out_blocks, dtype=jnp.int32)
    sources = positions[:, None] + block_shift
    inside = ((sources >= 0) & (sources < ext_width)).astype(jnp.float32)
    clipped = jnp.clip(sources, 0, ext_width - 1)
    group_size = 8

    def one_group(group_items):
        source_index, keep_mask, tile_index = group_items
        incoming_block = extended[source_index] * keep_mask[:, :, None, None]
        selected_entry = variant_table[tile_index]
        return jnp.einsum(
            "gskc,gsdc->gkd",
            incoming_block,
            selected_entry,
            precision=lax.Precision.HIGHEST,
            preferred_element_type=jnp.float32,
        )

    grouped = lax.map(
        one_group,
        (
            clipped.reshape(-1, group_size, slot_count),
            inside.reshape(-1, group_size, slot_count),
            table_index.reshape(-1, group_size, slot_count),
        ),
    )
    return grouped.reshape((out_blocks,) + extended.shape[1:])


def chebyshev(blocks, operate, bounds):
    half_width = (bounds[2] - bounds[1]) / 2
    centre = (bounds[2] + bounds[1]) / 2
    sigma_one = half_width / (bounds[0] - centre)
    sigma_base = 2 / sigma_one
    previous = blocks
    present_vectors = sigma_one / half_width * (operate(blocks) - centre * blocks)
    sigma_now = sigma_one
    for repeat in range(STEPS - 1):
        sigma_next = 1 / (sigma_base - sigma_now)
        advanced = (
            2 * sigma_next / half_width * (operate(present_vectors) - centre * present_vectors)
            - sigma_now * sigma_next * previous
        )
        previous = present_vectors
        present_vectors = advanced
        sigma_now = sigma_next
    return present_vectors


def on_device(vectors, tile_table, offsets, tile_ids, bounds):
    local_vecs = vectors.shape[0]
    local_rows = vectors.shape[1]
    block_count = local_rows // BLOCK
    blocks = vectors.reshape(local_vecs, block_count, BLOCK).transpose(1, 0, 2)
    metadata = jnp.concatenate([offsets, tile_ids], axis=1)
    flipped = tile_table.transpose(0, 2, 1)
    variant_table = jnp.concatenate([tile_table, flipped, (tile_table + flipped) / 2], axis=0)
    padded_meta = jnp.pad(metadata, ((R, R), (0, 0)))

    def apply_locally(field):
        padded = extended_2(field, (("rows", 0),), R)
        return band_product(padded, variant_table, padded_meta, R, block_count)

    filtered_blocks = chebyshev(blocks, apply_locally, bounds)
    filtered = filtered_blocks.transpose(1, 0, 2).reshape(local_vecs, local_rows)
    stacked = lax.all_to_all(filtered, "vec", split_axis=1, concat_axis=0, tiled=True)
    total_vecs = stacked.shape[0]
    all_rows = local_rows * lax.axis_size("rows")
    owner_count = lax.axis_size(("rows", "vec"))
    owned_rows = total_vecs // owner_count
    contract = (((1,), (1,)), ((), ()))
    partial_value = (
        lax.dot_general(
            stacked,
            stacked,
            contract,
            precision=lax.Precision.HIGHEST,
            preferred_element_type=jnp.float32,
        )
        / all_rows
    )
    summed_gram = lax.psum(partial_value, ("rows", "vec"))
    gram_matrix = lax.dynamic_slice_in_dim(
        summed_gram, lax.axis_index(("rows", "vec")) * owned_rows, owned_rows, 0
    )
    return (filtered, gram_matrix)


def solution(mesh):
    placed = (P("vec", "rows"), P(), P("rows", None), P("rows", None), P())
    return jax.shard_map(
        on_device,
        mesh=mesh,
        in_specs=placed,
        out_specs=(P("vec", "rows"), P(("rows", "vec"), None)),
        check_vma=False,
    )
```

profile of v0, /device:TPU:24, one launch (start us, length us, event | category | flops | bytes accessed | tf_op | source)
XLA Modules:
  0.0 477.2 jit_solution(14210082805207283505)
XLA Ops:
  8.0 1.7 collective-permute-start
  11.1 1.6 copy.55
  14.3 1.6 pad_maximum_fusion
  20.9 26.8 %while.40 = (s32[]{:T(128)}, f32[4,8,8,128]{3,2,1,0:T(8,128)}, s32[4,8,3]{1,0,2:T(4,128)S(1)}, f32[36,8,128]{2,1,0:T(8,128)S(1)}, f32[4,8,3]{1,2,0:T(4,128)S(1)}...) while((s32[]{:T(128)}, f32[4,8,8,128]{3,2,1,0:T(8,128)}, s32[4,8,3]{1,0,2:T(4,128)S(1)}, ...), condition=%wide.region_1.2_spmd, body=%wide.region_0.1_spmd.sunk | while | flops 37775504 | bytes 5057085 | solution.py:50
  21.1 1.8 gather_fusion
  23.8 3.8 fusion.44
  27.8 1.8 gather_fusion
  30.5 3.8 fusion.44
  34.5 1.8 gather_fusion
  37.2 3.8 fusion.44
  41.2 1.8 gather_fusion
  43.9 3.8 fusion.44
  49.3 5.2 %collective-permute-start.2 = (f32[2,8,128]{2,1,0:T(8,128)S(1)}, f32[2,8,128]{2,1,0:T(8,128)S(1)}, u32[]{:S(2)}, u32[]{:S(2)}) collective-permute-start(f32[2,8,128]{2,1,0:T(8,128)S(1)} %get-tuple-element.306), channel_id=1, source_target_pairs={{0,64},{64,128},{128,192},{192,256},{256,320},{320,384},{384,448},... | collective-permute-start | bytes 24584 | tf_op jit(solution)/shard_map/ppermute | solution.py:18
  55.9 2.8 collective-permute-done.3
  60.3 26.8 %while.41 = (s32[]{:T(128)}, f32[4,8,8,128]{3,2,1,0:T(8,128)}, s32[4,8,3]{1,0,2:T(4,128)S(1)}, f32[36,8,128]{2,1,0:T(8,128)S(1)}, f32[4,8,3]{1,2,0:T(4,128)S(1)}...) while((s32[]{:T(128)}, f32[4,8,8,128]{3,2,1,0:T(8,128)}, s32[4,8,3]{1,0,2:T(4,128)S(1)}, ...), condition=%wide.region_3.4_spmd, body=%wide.region_2.3_spmd.sunk | while | flops 37775504 | bytes 5057085 | solution.py:50
  60.5 1.8 gather_fusion.2
  63.2 3.8 fusion.47
  67.2 1.8 gather_fusion.2
  69.9 3.8 fusion.47
  73.9 1.8 gather_fusion.2
  76.6 3.8 fusion.47
  80.6 1.8 gather_fusion.2
  83.3 3.8 fusion.47
  88.8 4.3 collective-permute-start.4
  94.5 1.7 collective-permute-done.5
  97.8 26.8 %while.42 = (s32[]{:T(128)}, f32[4,8,8,128]{3,2,1,0:T(8,128)}, s32[4,8,3]{1,0,2:T(4,128)S(1)}, f32[36,8,128]{2,1,0:T(8,128)S(1)}, f32[4,8,3]{1,2,0:T(4,128)S(1)}...) while((s32[]{:T(128)}, f32[4,8,8,128]{3,2,1,0:T(8,128)}, s32[4,8,3]{1,0,2:T(4,128)S(1)}, ...), condition=%wide.region_5.6_spmd, body=%wide.region_4.5_spmd.sunk | while | flops 37775504 | bytes 5057085 | solution.py:50
  98.0 1.8 gather_fusion.4
  100.7 3.8 fusion.50
  104.7 1.8 gather_fusion.4
  107.4 3.8 fusion.50
  111.4 1.8 gather_fusion.4
  114.1 3.8 fusion.50
  118.1 1.8 gather_fusion.4
  120.8 3.8 fusion.50
  126.3 4.6 collective-permute-start.6
  132.3 1.7 collective-permute-done.7
  135.5 26.8 %while.43 = (s32[]{:T(128)}, f32[4,8,8,128]{3,2,1,0:T(8,128)}, s32[4,8,3]{1,0,2:T(4,128)S(1)}, f32[36,8,128]{2,1,0:T(8,128)S(1)}, f32[4,8,3]{1,2,0:T(4,128)S(1)}...) while((s32[]{:T(128)}, f32[4,8,8,128]{3,2,1,0:T(8,128)}, s32[4,8,3]{1,0,2:T(4,128)S(1)}, ...), condition=%wide.region_7.8_spmd, body=%wide.region_6.7_spmd.sunk | while | flops 37775504 | bytes 5057085 | solution.py:50
  135.7 1.8 gather_fusion.6
  138.4 3.8 fusion.53
  142.4 1.8 gather_fusion.6
  145.1 3.8 fusion.53
  149.1 1.8 gather_fusion.6
  151.8 3.8 fusion.53
  155.8 1.8 gather_fusion.6
  158.5 3.8 fusion.53
  163.9 30.0 %all_to_all.19 = f32[64,1,512]{2,1,0:T(1,128)S(1)} all-to-all(f32[64,1,512]{2,1,0:T(1,128)S(1)} %reshape.378), channel_id=1, replica_groups=mesh['rows'=8,'vec'=64] {'vec'}, dimensions={0} | all-to-all | bytes 262144 | tf_op jit(solution)/shard_map/all_to_all | solution.py:97
  195.4 2.0 convolution_multiply_fusion
  197.4 271.7 %all-reduce.2.cloned.1.call-done = f32[512,512]{1,0:T(8,128)} async-done(((f32[512,512]{1,0:T(8,128)}), f32[512,512]{1,0:T(8,128)}) %all-reduce.2.cloned.1.call-update) | async-done | bytes 1048592 | tf_op jit(solution)/shard_map/psum | solution.py:113
  (228 shorter events, 39.6 us)
Async XLA Ops:
  7.2 5.5 %copy-start = (f32[16,128,128]{2,1,0:T(8,128)S(1)}, f32[16,128,128]{2,1,0:T(8,128)}, u32[]{:S(2)}) copy-start(f32[16,128,128]{2,1,0:T(8,128)} %param.14) | copy-start | bytes 3145732
  7.2 461.9 %all-reduce.2.cloned.1.call-start = ((), (), s32[]{:S(2)}) async-start(), calls=%async_computation.1 | async-start | bytes 2097152 | tf_op jit(solution)/shard_map/psum | solution.py:113
  8.0 12.2 %collective-permute-start = (f32[2,8,128]{2,1,0:T(8,128)S(1)}, f32[2,8,128]{2,1,0:T(8,128)S(1)}, u32[]{:S(2)}, u32[]{:S(2)}) collective-permute-start(f32[2,8,128]{2,1,0:T(8,128)S(1)} %get-tuple-element.308), channel_id=1, source_target_pairs={{0,64},{64,128},{128,192},{192,256},{256,320},{320,384},{384,448},... | collective-permute-start | bytes 24584 | tf_op jit(solution)/shard_map/ppermute | solution.py:18
  9.8 10.5 %collective-permute-start.1 = (f32[2,8,128]{2,1,0:T(8,128)S(1)}, f32[2,8,128]{2,1,0:T(8,128)S(1)}, u32[]{:S(2)}, u32[]{:S(2)}) collective-permute-start(f32[2,8,128]{2,1,0:T(8,128)S(1)} %get-tuple-element.309), channel_id=1, source_target_pairs={{64,0},{128,64},{192,128},{256,192},{320,256},{384,320},{448,384},... | collective-permute-start | bytes 24584 | tf_op jit(solution)/shard_map/ppermute | solution.py:19
  12.6 1.0 copy-start.2
  12.6 1.0 copy-start.9
  12.7 1.0 copy-start.11
  12.7 1.6 copy-start.1
  14.3 1.6 copy-start.10
  14.3 5.9 %copy-start.3 = (f32[8,4096]{1,0:T(8,128)S(1)}, f32[8,4096]{1,0:T(8,128)}, u32[]{:S(2)}) copy-start(f32[8,4096]{1,0:T(8,128)} %param.13) | copy-start | bytes 393220
  48.6 0.7 copy-start.7
  49.3 6.7 %collective-permute-start.2 = (f32[2,8,128]{2,1,0:T(8,128)S(1)}, f32[2,8,128]{2,1,0:T(8,128)S(1)}, u32[]{:S(2)}, u32[]{:S(2)}) collective-permute-start(f32[2,8,128]{2,1,0:T(8,128)S(1)} %get-tuple-element.306), channel_id=1, source_target_pairs={{0,64},{64,128},{128,192},{192,256},{256,320},{320,384},{384,448},... | collective-permute-start | bytes 24584 | tf_op jit(solution)/shard_map/ppermute | solution.py:18
  54.4 4.3 collective-permute-start.3
  88.2 0.7 copy-start.4
  88.8 5.7 %collective-permute-start.4 = (f32[2,8,128]{2,1,0:T(8,128)S(1)}, f32[2,8,128]{2,1,0:T(8,128)S(1)}, u32[]{:S(2)}, u32[]{:S(2)}) collective-permute-start(f32[2,8,128]{2,1,0:T(8,128)S(1)} %get-tuple-element.304), channel_id=1, source_target_pairs={{0,64},{64,128},{128,192},{192,256},{256,320},{320,384},{384,448},... | collective-permute-start | bytes 24584 | tf_op jit(solution)/shard_map/ppermute | solution.py:18
  93.1 3.1 collective-permute-start.5
  125.7 0.6 copy-start.6
  126.3 6.0 %collective-permute-start.6 = (f32[2,8,128]{2,1,0:T(8,128)S(1)}, f32[2,8,128]{2,1,0:T(8,128)S(1)}, u32[]{:S(2)}, u32[]{:S(2)}) collective-permute-start(f32[2,8,128]{2,1,0:T(8,128)S(1)} %get-tuple-element.302), channel_id=1, source_target_pairs={{0,64},{64,128},{128,192},{192,256},{256,320},{320,384},{384,448},... | collective-permute-start | bytes 24584 | tf_op jit(solution)/shard_map/ppermute | solution.py:18
  130.9 3.1 collective-permute-start.7
  135.5 26.8 %copy-start.5 = (f32[32,8,128]{2,1,0:T(8,128)S(1)}, f32[32,8,128]{2,1,0:T(8,128)}, u32[]{:S(2)}) copy-start(f32[32,8,128]{2,1,0:T(8,128)} %copy-done.4) | copy-start | bytes 393220
  163.3 34.0 %copy-start.8 = (f32[32,8,128]{2,1,0:T(8,128)}, f32[32,8,128]{2,1,0:T(8,128)S(1)}, u32[]{:S(2)}) copy-start(f32[32,8,128]{2,1,0:T(8,128)S(1)} %fusion.14) | copy-start | bytes 393220
Sparse Core Ops, SparseCore 0:
  197.5 271.5 all-reduce.1
where the time goes:
time: 478 us; the launch traced here: 477 us
  waiting for transfers between devices  278 us (58%)
  matrix products  62.9 us (13%)
  local copies, waits for them, and re-layouts  57.2 us (12%)
  blocking collectives  30 us (6%)
  starting transfers between devices  21 us (4%)
  between operations  18.1 us (4%)
  other arithmetic  9.89 us (2%)
    psum x1, waiting for transfers between devices, on_device(): summed_gram = lax.psum(partial_value, ('rows', 'vec'))  272 us
    dot_general x16, matrix products, one_group(): jnp.einsum('gskc,gsdc->gkd', incoming_block, selected_entry, precision=la...  60.9 us
    all_to_all x1, blocking collectives, on_device(): lax.all_to_all(filtered, 'vec', split_axis=1, concat_axis=0, tiled=True)  30 us
    gather x16, local copies, waits for them, and re-layouts, one_group(): selected_entry = variant_table[tile_index]  29.5 us
    ppermute x4, starting transfers between devices, extended_2(): before = lax.ppermute(last, axis, up)  15.8 us
  transfers between devices with their start and end apart: 9, of which 4 were waited for; matrix products, arithmetic and copies ran while one was open for 1% of the time, Pallas kernels for 0%

commit v1 on v0

--- a/solution.py
+++ b/solution.py
@@ -110,7 +110,7 @@
         )
         / all_rows
     )
-    summed_gram = lax.psum(partial_value, ("rows", "vec"))
+    summed_gram = lax.psum(lax.psum(partial_value, "rows"), "vec")
     gram_matrix = lax.dynamic_slice_in_dim(
         summed_gram, lax.axis_index(("rows", "vec")) * owned_rows, owned_rows, 0
     )

time: 478 us -> 1130 us (2.36)
  the two profiles are of different devices: /device:TPU:24 before, /device:TPU:8 now
where the time goes in v1:
time: 1130 us
  waiting for transfers between devices  932 us (82%)
  matrix products  62.9 us (6%)
  local copies, waits for them, and re-layouts  56.3 us (5%)
  blocking collectives  31.1 us (3%)
  starting transfers between devices  21 us (2%)
  between operations  18 us (2%)
    psum x2, waiting for transfers between devices, on_device(): summed_gram = lax.psum(lax.psum(partial_value, 'rows'), 'vec')  927 us
    dot_general x16, matrix products, one_group(): jnp.einsum('gskc,gsdc->gkd', incoming_block, selected_entry, precision=la...  61 us
    all_to_all x1, blocking collectives, on_device(): lax.all_to_all(filtered, 'vec', split_axis=1, concat_axis=0, tiled=True)  31.1 us
    gather x16, local copies, waits for them, and re-layouts, one_group(): selected_entry = variant_table[tile_index]  29.4 us
  transfers between devices with their start and end apart: 10, of which 5 were waited for; matrix products, arithmetic and copies ran while one was open for 0% of the time, Pallas kernels for 0%

profile of v1, /device:TPU:8, one launch (start us, length us, event | category | flops | bytes accessed | tf_op | source)
XLA Modules:
  0.0 1131.3 jit_solution(7140984587475921914)
XLA Ops:
  8.0 1.7 collective-permute-start
  11.1 1.6 copy.55
  14.3 1.5 pad_maximum_fusion
  20.6 26.7 %while.40 = (s32[]{:T(128)}, f32[4,8,8,128]{3,2,1,0:T(8,128)}, s32[4,8,3]{1,0,2:T(4,128)S(1)}, f32[36,8,128]{2,1,0:T(8,128)S(1)}, f32[4,8,3]{1,2,0:T(4,128)S(1)}...) while((s32[]{:T(128)}, f32[4,8,8,128]{3,2,1,0:T(8,128)}, s32[4,8,3]{1,0,2:T(4,128)S(1)}, ...), condition=%wide.region_1.2_spmd, body=%wide.region_0.1_spmd.sunk | while | flops 37775504 | bytes 5057085 | solution.py:50
  20.8 1.8 gather_fusion
  23.5 3.8 fusion.44
  27.5 1.8 gather_fusion
  30.2 3.8 fusion.44
  34.2 1.8 gather_fusion
  36.9 3.8 fusion.44
  40.9 1.8 gather_fusion
  43.6 3.8 fusion.44
  48.3 5.2 collective-permute-start.2
  55.6 2.4 collective-permute-done.3
  59.6 26.8 %while.41 = (s32[]{:T(128)}, f32[4,8,8,128]{3,2,1,0:T(8,128)}, s32[4,8,3]{1,0,2:T(4,128)S(1)}, f32[36,8,128]{2,1,0:T(8,128)S(1)}, f32[4,8,3]{1,2,0:T(4,128)S(1)}...) while((s32[]{:T(128)}, f32[4,8,8,128]{3,2,1,0:T(8,128)}, s32[4,8,3]{1,0,2:T(4,128)S(1)}, ...), condition=%wide.region_3.4_spmd, body=%wide.region_2.3_spmd.sunk | while | flops 37775504 | bytes 5057085 | solution.py:50
  59.8 1.8 gather_fusion.2
  62.5 3.8 fusion.47
  66.4 1.8 gather_fusion.2
  69.1 3.8 fusion.47
  73.1 1.8 gather_fusion.2
  75.8 3.8 fusion.47
  79.8 1.8 gather_fusion.2
  82.5 3.8 fusion.47
  87.4 4.3 collective-permute-start.4
  96.5 26.8 %while.42 = (s32[]{:T(128)}, f32[4,8,8,128]{3,2,1,0:T(8,128)}, s32[4,8,3]{1,0,2:T(4,128)S(1)}, f32[36,8,128]{2,1,0:T(8,128)S(1)}, f32[4,8,3]{1,2,0:T(4,128)S(1)}...) while((s32[]{:T(128)}, f32[4,8,8,128]{3,2,1,0:T(8,128)}, s32[4,8,3]{1,0,2:T(4,128)S(1)}, ...), condition=%wide.region_5.6_spmd, body=%wide.region_4.5_spmd.sunk | while | flops 37775504 | bytes 5057085 | solution.py:50
  96.7 1.8 gather_fusion.4
  99.3 3.8 fusion.50
  103.3 1.8 gather_fusion.4
  106.0 3.8 fusion.50
  110.0 1.8 gather_fusion.4
  112.7 3.8 fusion.50
  116.7 1.8 gather_fusion.4
  119.4 3.8 fusion.50
  124.3 4.5 collective-permute-start.6
  130.3 1.7 collective-permute-done.7
  133.5 26.8 %while.43 = (s32[]{:T(128)}, f32[4,8,8,128]{3,2,1,0:T(8,128)}, s32[4,8,3]{1,0,2:T(4,128)S(1)}, f32[36,8,128]{2,1,0:T(8,128)S(1)}, f32[4,8,3]{1,2,0:T(4,128)S(1)}...) while((s32[]{:T(128)}, f32[4,8,8,128]{3,2,1,0:T(8,128)}, s32[4,8,3]{1,0,2:T(4,128)S(1)}, ...), condition=%wide.region_7.8_spmd, body=%wide.region_6.7_spmd.sunk | while | flops 37775504 | bytes 5057085 | solution.py:50
  133.7 1.8 gather_fusion.6
  136.4 3.8 fusion.53
  140.4 1.8 gather_fusion.6
  143.1 3.8 fusion.53
  147.1 1.8 gather_fusion.6
  149.8 3.8 fusion.53
  153.8 1.8 gather_fusion.6
  156.5 3.8 fusion.53
  161.8 31.1 %all_to_all.19 = f32[64,1,512]{2,1,0:T(1,128)S(1)} all-to-all(f32[64,1,512]{2,1,0:T(1,128)S(1)} %reshape.378), channel_id=1, replica_groups=mesh['rows'=8,'vec'=64] {'vec'}, dimensions={0} | all-to-all | bytes 262144 | tf_op jit(solution)/shard_map/all_to_all | solution.py:97
  194.5 2.0 convolution_multiply_fusion
  196.5 74.7 %all-reduce.3.cloned.1.call-done = f32[512,512]{1,0:T(8,128)} async-done(((f32[512,512]{1,0:T(8,128)}), f32[512,512]{1,0:T(8,128)}) %all-reduce.3.cloned.1.call-update) | async-done | bytes 1048592 | tf_op jit(solution)/shard_map/psum | solution.py:113
  271.2 851.9 %all-reduce.5.cloned.1.call-done = f32[512,512]{1,0:T(8,128)} async-done(((f32[512,512]{1,0:T(8,128)}), f32[512,512]{1,0:T(8,128)}) %all-reduce.5.cloned.1.call-update) | async-done | bytes 1048592 | tf_op jit(solution)/shard_map/psum | solution.py:113
  (235 shorter events, 40.2 us)
Async XLA Ops:
  7.2 5.5 copy-start
  7.2 264.0 %all-reduce.3.cloned.1.call-start = ((), (), s32[]{:S(2)}) async-start(), calls=%async_computation.1 | async-start | bytes 2097152 | tf_op jit(solution)/shard_map/psum | solution.py:113
  8.0 11.9 %collective-permute-start = (f32[2,8,128]{2,1,0:T(8,128)S(1)}, f32[2,8,128]{2,1,0:T(8,128)S(1)}, u32[]{:S(2)}, u32[]{:S(2)}) collective-permute-start(f32[2,8,128]{2,1,0:T(8,128)S(1)} %get-tuple-element.308), channel_id=1, source_target_pairs={{0,64},{64,128},{128,192},{192,256},{256,320},{320,384},{384,448},... | collective-permute-start | bytes 24584 | tf_op jit(solution)/shard_map/ppermute | solution.py:18
  9.8 10.2 collective-permute-start.1
  12.6 1.0 copy-start.2
  12.6 1.0 copy-start.11
  12.7 1.0 copy-start.13
  12.7 1.6 copy-start.1
  14.3 1.5 copy-start.12
  14.3 5.7 copy-start.3
  48.3 6.7 copy-start.7
  48.3 6.7 collective-permute-start.2
  53.5 4.4 collective-permute-start.3
  55.0 0.6 copy-start.9
  87.4 5.7 copy-start.4
  87.4 5.7 collective-permute-start.4
  91.7 3.2 collective-permute-start.5
  93.1 0.6 copy-start.10
  124.3 6.0 copy-start.6
  124.3 5.9 collective-permute-start.6
  128.9 3.1 collective-permute-start.7
  133.5 26.8 %copy-start.5 = (f32[32,8,128]{2,1,0:T(8,128)S(1)}, f32[32,8,128]{2,1,0:T(8,128)}, u32[]{:S(2)}) copy-start(f32[32,8,128]{2,1,0:T(8,128)} %copy-done.4) | copy-start | bytes 393220
  161.3 35.1 %copy-start.8 = (f32[32,8,128]{2,1,0:T(8,128)}, f32[32,8,128]{2,1,0:T(8,128)S(1)}, u32[]{:S(2)}) copy-start(f32[32,8,128]{2,1,0:T(8,128)S(1)} %fusion.14) | copy-start | bytes 393220
  196.5 926.7 %all-reduce.5.cloned.1.call-start = ((), (), s32[]{:S(2)}) async-start(), calls=%async_computation.2 | async-start | bytes 2097152 | tf_op jit(solution)/shard_map/psum | solution.py:113
Sparse Core Ops, SparseCore 0:
  196.6 74.5 all-reduce.2
  274.1 849.0 all-reduce.4
